TPU v7x, 32 devices: a whole 2x2x4 slice. The times are simulated.
32 devices in a mesh: expert: 4 (over x, core), ctx: 2 (over y), tensor: 4 (over z).
Axes of the slice: x: 2, y: 2, z: 4, core: 2. Of those that a mesh axis runs over, the one named last changes fastest.
Arguments:
- tokens: bfloat16 [64, 6144], P('expert', 'tensor'), may hold values from -6 to 6
- expert_ids: int32 [64, 2], P('expert'), may hold values from 0 to 3, all different within a row; in each aligned block of 8 rows (0 to 7, 8 to 15, ...) at most 4 rows name the same one
- route_gates: float32 [64, 2], P('expert'), may hold values from 0.2 to 1
- up_weight: bfloat16 [4, 12288, 6144], P('expert', 'ctx', 'tensor'), may hold values from -0.078125 to 0.078125
- down_weight: bfloat16 [4, 12288, 6144], P('expert', 'ctx', 'tensor'), may hold values from -0.0546875 to 0.0546875
Outputs:
- mixed: bfloat16 [64, 6144], P(('expert', 'ctx'), 'tensor')
Inputs may be any that keep to these rules, and one draw needn't show every extreme that they name: `expert_ids`: each token names 2 different experts. In each aligned block of 8 tokens at most 4 choices name one expert, and in some block one expert is named exactly 4 times. Every expert is named somewhere.
All inputs are finite; a program needn't handle non-finite values.
Results may differ from a plain program's by a relative error of at most 0.0057.
Values may be sent and summed in bfloat16 or wider, within the bound.
No kernel may reach another device: no remote copies, remote signals or barrier semaphores. Data moves between devices by JAX's collectives and lax.ppermute only.
A program may use at most 64 MiB of HBM per device.

v0:
```python
import jax
import jax.numpy as jnp
from jax import lax
from jax.sharding import PartitionSpec as P


def choice_slots(expert_ids, block_len, expert_count):
    top_count = expert_ids.shape[1]
    per_block = expert_ids.reshape(-1, block_len * top_count)
    marked = (
        per_block[:, :, None] == jnp.arange(expert_count, dtype=jnp.int32)[None, None, :]
    ).astype(jnp.int32)
    earlier = jnp.cumsum(marked, axis=1) - marked
    return jnp.sum(earlier * marked, axis=2).reshape(-1, top_count)


def local(tokens, expert_ids, route_gates, up_weight, down_weight):
    ctx_count = lax.axis_size("ctx")
    expert_count = lax.axis_size("expert")
    group_len = tokens.shape[0]
    width_local = tokens.shape[1]
    block_len = group_len // ctx_count
    capacity = block_len // 2
    per_expert = ctx_count * capacity
    ctx_index = lax.axis_index("ctx")
    slot_ids = choice_slots(expert_ids, block_len, expert_count)
    block_of = (jnp.arange(group_len, dtype=jnp.int32) // block_len)[:, None]
    dest_index = expert_ids * per_expert + block_of * capacity + slot_ids
    slot_range = jnp.arange(expert_count * per_expert, dtype=jnp.int32)
    marked = jnp.sum(
        (dest_index[None, :, :] == slot_range[:, None, None]).astype(jnp.int32), axis=2
    )
    outgoing = jnp.dot(marked.astype(jnp.bfloat16), tokens, preferred_element_type=jnp.float32)
    outgoing = outgoing.astype(jnp.bfloat16).reshape(expert_count, per_expert, width_local)
    arrived = lax.all_to_all(outgoing, "expert", split_axis=0, concat_axis=0, tiled=True)
    row_data = arrived.reshape(-1, width_local)
    up_local = up_weight[0]
    down_local = down_weight[0]
    before_act = lax.dot_general(
        row_data, up_local, (((1,), (1,)), ((), ())), preferred_element_type=jnp.float32
    )
    share = lax.psum_scatter(before_act, "tensor", scatter_dimension=0, tiled=True)
    hidden = jnp.square(jnp.maximum(share, 0.0)).astype(jnp.bfloat16)
    projected = jnp.dot(
        lax.all_gather(hidden, "tensor", axis=0, tiled=True),
        down_local,
        preferred_element_type=jnp.float32,
    )
    by_block = projected.reshape(expert_count, ctx_count, capacity, width_local)
    totals = lax.psum(by_block, "ctx")
    own_rows = lax.dynamic_index_in_dim(totals, ctx_index, 1, keepdims=False)
    returned = lax.all_to_all(
        own_rows.astype(jnp.bfloat16), "expert", split_axis=0, concat_axis=0, tiled=True
    )
    flattened = returned.reshape(-1, width_local)
    first_row = ctx_index * block_len
    own_ids = lax.dynamic_slice_in_dim(expert_ids, first_row, block_len, 0)
    own_slots = lax.dynamic_slice_in_dim(slot_ids, first_row, block_len, 0)
    own_gates = lax.dynamic_slice_in_dim(route_gates, first_row, block_len, 0)
    row_index = own_ids * capacity + own_slots
    picked = jnp.take(flattened, row_index, axis=0).astype(jnp.float32)
    mixed = jnp.sum(own_gates[:, :, None] * picked, axis=1)
    return mixed.astype(jnp.bfloat16)


def solution(mesh):
    in_specs = (
        P("expert", "tensor"),
        P("expert", None),
        P("expert", None),
        P("expert", "ctx", "tensor"),
        P("expert", "ctx", "tensor"),
    )
    out_specs = P(("expert", "ctx"), "tensor")
    return jax.shard_map(local, mesh=mesh, in_specs=in_specs, out_specs=out_specs, check_vma=False)
```

profile of v0, /device:TPU:0, one launch (start us, length us, event | category | flops | bytes accessed | tf_op | source)
XLA Modules:
  0.0 106.3 jit_solution(8248955880566829928)
XLA Ops:
  6.5 0.0 copy-start
  6.5 0.0 reduce-scatter.2.cloned.1.call-start
  6.5 0.8 copy.26
  7.3 0.1 eq.28
  7.4 0.1 fusion.7
  7.5 0.2 select_reduce_fusion
  7.7 0.1 reshape.38
  7.8 0.1 copy.28
  7.9 0.7 add_add_fusion
  8.6 0.1 convert_reduce_fusion
  8.6 0.0 copy-done
  8.6 0.2 fusion.4
  8.8 8.3 %all_to_all.10 = bf16[4,8,1536]{2,1,0:T(8,128)(2,1)S(1)} all-to-all(bf16[4,8,1536]{2,1,0:T(8,128)(2,1)S(1)} %fusion.4), channel_id=1, replica_groups=mesh['expert'=4,'ctx'=2,'tensor'=4] {'expert'}, dimensions={0} | all-to-all | bytes 196608 | tf_op jit(solution)/shard_map/all_to_all | solution.py:35
  17.2 0.0 copy-start.1
  17.2 12.8 %fusion.2 = f32[32,6144]{1,0:T(8,128)} fusion(bf16[1,6144,1536]{2,1,0:T(8,128)(2,1)} %param.8, bf16[4,8,1536]{2,1,0:T(8,128)(2,1)S(1)} %all_to_all.10), kind=kOutput, calls=%fused_computation.3 | convolution fusion | flops 603979776 | bytes 19759104 | tf_op jit(solution)/shard_map/dot_general | solution.py:39
  30.0 0.0 reduce-scatter.2.cloned.1.call-update
  30.0 0.1 reshape.44
  30.1 23.5 %reduce-scatter.2.cloned.1.call-done = f32[8,6144]{1,0:T(8,128)} async-done(((f32[32,6144]{1,0:T(8,128)}), f32[8,6144]{1,0:T(8,128)}) %reduce-scatter.2.cloned.1.call-update) | async-done | bytes 196624 | tf_op jit(solution)/shard_map/reduce_scatter | solution.py:42
  53.6 0.9 multiply_convert_fusion
  54.6 15.3 %all_gather.3 = bf16[32,6144]{1,0:T(8,128)(2,1)S(1)} all-gather(bf16[8,6144]{1,0:T(8,128)(2,1)S(1)} %multiply_convert_fusion), channel_id=1, replica_groups=mesh['expert'=4,'ctx'=2,'tensor'=4] {'tensor'}, dimensions={0}, use_global_device_ids=true | all-gather | bytes 491520 | tf_op jit(solution)/shard_map/all_gather | solution.py:45
  69.8 0.1 dot_general.13
  70.0 9.6 %fusion = f32[4,2,4,1536]{3,2,1,0:T(4,128)S(1)} fusion(bf16[4,2,4,6144]{3,2,1,0:T(4,128)(2,1)S(1)} %dot_general.13, bf16[1,6144,1536]{2,1,0:T(8,128)(2,1)} %param.9), kind=kOutput, calls=%fused_computation.1 | convolution fusion | flops 603979776 | bytes 19464192 | tf_op jit(solution)/shard_map/dot_general | solution.py:44
  79.6 10.5 %all-reduce.1 = bf16[4,2,4,1536]{3,2,1,0:T(4,128)(2,1)S(1)} all-reduce(f32[4,2,4,1536]{3,2,1,0:T(4,128)S(1)} %fusion), channel_id=1, replica_groups=mesh['expert'=4,'ctx'=2,'tensor'=4] {'ctx'}, use_global_device_ids=true, to_apply=%region_4.5 | all-reduce | flops 49152 | bytes 294912 | tf_op jit(solution)/shard_map/psum | solution.py:50
  90.0 0.6 fusion.6
  90.7 3.3 %all-to-all-start.1 = ((bf16[4,4,1536]{2,1,0:T(4,128)(2,1)}), bf16[4,4,1536]{2,1,0:T(4,128)(2,1)S(1)}, u32[]{:S(2)}, u32[]{:S(2)}) async-start(bf16[4,4,1536]{2,1,0:T(4,128)(2,1)} %fusion.6), calls=%async_computation.2 | async-start | bytes 98304 | tf_op jit(solution)/shard_map/all_to_all | solution.py:52
  93.9 0.0 copy-done.1
  93.9 0.1 constant_dynamic-slice_fusion
  94.0 0.1 copy.25
  94.1 3.8 %all-to-all-done.1 = bf16[4,4,1536]{2,1,0:T(4,128)(2,1)S(1)} async-done(((bf16[4,4,1536]{2,1,0:T(4,128)(2,1)}), bf16[4,4,1536]{2,1,0:T(4,128)(2,1)S(1)}, u32[]{:S(2)}, u32[]{:S(2)}) %all-to-all-start.1) | async-done | bytes 49184 | tf_op jit(solution)/shard_map/all_to_all | solution.py:52
  98.0 0.6 gather_fusion
  98.6 0.8 multiply_reduce_fusion
  (6 shorter events, 0.1 us)
Async XLA Ops:
  6.5 2.1 %copy-start = (bf16[16,1536]{1,0:T(8,128)(2,1)S(1)}, bf16[16,1536]{1,0:T(8,128)(2,1)}, u32[]{:S(2)}) copy-start(bf16[16,1536]{1,0:T(8,128)(2,1)} %param.5) | copy-start | bytes 147460
  6.5 47.1 %reduce-scatter.2.cloned.1.call-start = ((), (), s32[]{:S(2)}) async-start(), calls=%async_computation.3 | async-start | bytes 983040 | tf_op jit(solution)/shard_map/reduce_scatter | solution.py:42
  17.2 76.8 %copy-start.1 = (f32[16,2]{0,1:T(2,128)S(1)}, f32[16,2]{0,1:T(2,128)}, u32[]{:S(2)}) copy-start(f32[16,2]{0,1:T(2,128)} %param.7) | copy-start | bytes 388
  90.7 7.3 %all-to-all-start.1 = ((bf16[4,4,1536]{2,1,0:T(4,128)(2,1)}), bf16[4,4,1536]{2,1,0:T(4,128)(2,1)S(1)}, u32[]{:S(2)}, u32[]{:S(2)}) async-start(bf16[4,4,1536]{2,1,0:T(4,128)(2,1)} %fusion.6), calls=%async_computation.2 | async-start | bytes 98304 | tf_op jit(solution)/shard_map/all_to_all | solution.py:52
Sparse Core Ops, SparseCore 0:
  30.1 23.4 reduce-scatter.1
where the time goes:
time: 107 us; the launch traced here: 106 us
  blocking collectives  34 us (32%)
  waiting for transfers between devices  27.3 us (26%)
  matrix products  22.6 us (21%)
  between operations  13.5 us (13%)
  starting transfers between devices  3.27 us (3%)
  other arithmetic  2.87 us (3%)
  local copies, waits for them, and re-layouts  2.69 us (3%)
    reduce_scatter x1, waiting for transfers between devices, local(): lax.psum_scatter(before_act, 'tensor', scatter_dimension=0, tiled=True)  23.5 us
    all_gather x1, blocking collectives, local(): lax.all_gather(hidden, 'tensor', axis=0, tiled=True)  15.3 us
    dot_general x1, matrix products, local(): lax.dot_general(row_data, up_local, (((1,), (1,)), ((), ())), preferred_e...  12.8 us
    psum x1, blocking collectives, local(): totals = lax.psum(by_block, 'ctx')  10.5 us
    dot_general x1, matrix products, local(): jnp.dot(lax.all_gather(hidden, 'tensor', axis=0, tiled=True), down_local,...  9.55 us
    all_to_all x1, blocking collectives, local(): lax.all_to_all(outgoing, 'expert', split_axis=0, concat_axis=0, tiled=True)  8.33 us
    all_to_all x1, waiting for transfers between devices, local(): lax.all_to_all(own_rows.astype(jnp.bfloat16), 'expert', split_axis=0, con...  3.83 us
    all_to_all x1, starting transfers between devices, local(): lax.all_to_all(own_rows.astype(jnp.bfloat16), 'expert', split_axis=0, con...  3.27 us
  transfers between devices with their start and end apart: 2, of which 2 were waited for; matrix products, arithmetic and copies ran while one was open for 0% of the time, Pallas kernels for 0%

commit v1 on v0

v1 whole, which is shorter than its diff:
```python
import functools

import jax
import jax.numpy as jnp
from jax import lax
from jax.experimental import pallas as pl
from jax.experimental.pallas import tpu as pltpu
from jax.sharding import PartitionSpec as P

VMEM = pl.BlockSpec(memory_space=pltpu.VMEM)
MIB = 1 << 20
AHEAD = 1 << 34


def shift_of(size):
    return size.bit_length() - 1


def vmem_call(body, args, outs, name, flops=0, moved=0, limit=4 * MIB):
    return pl.pallas_call(
        body,
        in_specs=[VMEM] * len(args),
        out_specs=jax.tree.map(lambda _: VMEM, outs),
        out_shape=outs,
        name=name,
        cost_estimate=pl.CostEstimate(flops=flops, transcendentals=0, bytes_accessed=moved),
        compiler_params=pltpu.CompilerParams(vmem_limit_bytes=limit),
    )(*args)


def named_before(ids, expert_row, block_len):
    count = ids.shape[0]
    first = ids[:, 0:1] == expert_row
    second = ids[:, 1:2] == expert_row
    names = jnp.where(first | second, 1.0, 0.0)
    row = lax.broadcasted_iota(jnp.int32, (count, count), 0)
    col = lax.broadcasted_iota(jnp.int32, (count, count), 1)
    shift = shift_of(block_len)
    earlier = (col < row) & (lax.shift_right_logical(row, shift) == lax.shift_right_logical(col, shift))
    slot = jnp.dot(
        jnp.where(earlier, 1.0, 0.0).astype(jnp.bfloat16),
        names.astype(jnp.bfloat16),
        preferred_element_type=jnp.float32,
    )
    return first, second, names, slot


def dispatch_body(tokens_ref, ids_ref, *out_refs, block_len, capacity, per_expert):
    ids = ids_ref[...]
    group_len = ids.shape[0]
    lanes = per_expert * len(out_refs)
    lane = lax.broadcasted_iota(jnp.int32, (1, lanes), 1)
    expert_row = lax.axis_index("expert") ^ lax.shift_right_logical(lane, shift_of(per_expert))
    _, _, names, slot = named_before(ids, expert_row, block_len)
    want_slot = (lane & (capacity - 1)).astype(jnp.float32)
    want_block = lax.shift_right_logical(lane, shift_of(capacity)) & (per_expert // capacity - 1)
    token = lax.broadcasted_iota(jnp.int32, (group_len, lanes), 0)
    hit = (names > 0) & (slot == want_slot) & (lax.shift_right_logical(token, shift_of(block_len)) == want_block)
    rows = lax.dot_general(
        jnp.where(hit, 1.0, 0.0).astype(jnp.bfloat16),
        tokens_ref[...],
        (((0,), (0,)), ((), ())),
        preferred_element_type=jnp.float32,
    ).astype(jnp.bfloat16)
    for k, ref in enumerate(out_refs):
        ref[...] = rows[k * per_expert:(k + 1) * per_expert]


def up_body(*refs, step, chunk):
    *row_refs, up_ref, out_ref = refs
    rows = jnp.concatenate([ref[...] for ref in row_refs], axis=0)
    start = pl.multiple_of((lax.axis_index("tensor") ^ step) * chunk, chunk)
    out_ref[...] = lax.dot_general(
        rows, up_ref[pl.ds(start, chunk), :], (((1,), (1,)), ((), ())), preferred_element_type=jnp.float32
    ).astype(out_ref.dtype)


def act_body(*refs):
    *part_refs, out_ref = refs
    total = part_refs[0][...].astype(jnp.float32)
    for ref in part_refs[1:]:
        total = total + ref[...].astype(jnp.float32)
    out_ref[...] = jnp.square(jnp.maximum(total, 0.0)).astype(jnp.bfloat16)


def down_body(*refs, step, chunk):
    hidden_ref, down_ref, *prior, out_ref = refs
    start = pl.multiple_of((lax.axis_index("tensor") ^ step) * chunk, chunk)
    total = jnp.dot(hidden_ref[...], down_ref[pl.ds(start, chunk), :], preferred_element_type=jnp.float32)
    if prior:
        total = total + prior[0][...]
    out_ref[...] = total


def last_body(hidden_ref, down_ref, prior_ref, out_ref, *, step, chunk, ctx_count, capacity):
    start = pl.multiple_of((lax.axis_index("tensor") ^ step) * chunk, chunk)
    total = prior_ref[...] + jnp.dot(
        hidden_ref[...], down_ref[pl.ds(start, chunk), :], preferred_element_type=jnp.float32
    )
    mine = lax.axis_index("expert")
    for piece in range(total.shape[0] // capacity):
        k, b = piece // ctx_count, piece % ctx_count
        dest = (mine ^ k) * ctx_count + b
        out_ref[dest] = total[piece * capacity:(piece + 1) * capacity].astype(out_ref.dtype)


def mix_body(back_ref, ids_ref, gates_ref, out_ref, *, block_len, capacity, ctx_count):
    lanes_all = back_ref.shape[0]
    expert_count = lanes_all // ctx_count
    picked = []
    for e in range(expert_count):
        total = back_ref[e * ctx_count].astype(jnp.float32)
        for c in range(1, ctx_count):
            total = total + back_ref[e * ctx_count + c].astype(jnp.float32)
        picked.append(total)
    rows = jnp.concatenate(picked, axis=0).astype(jnp.bfloat16)
    start = pl.multiple_of(lax.axis_index("ctx") * block_len, block_len)
    ids = ids_ref[pl.ds(start, block_len), :]
    gates = gates_ref[pl.ds(start, block_len), :]
    lane = lax.broadcasted_iota(jnp.int32, (1, expert_count * capacity), 1)
    first, second, _, slot = named_before(ids, lax.shift_right_logical(lane, shift_of(capacity)), block_len)
    here = slot == (lane & (capacity - 1)).astype(jnp.float32)
    mixed = 0.0
    for which, gate in ((first, gates[:, 0:1]), (second, gates[:, 1:2])):
        pick = jnp.where(which & here, 1.0, 0.0).astype(jnp.bfloat16)
        mixed = mixed + gate * jnp.dot(pick, rows, preferred_element_type=jnp.float32)
    out_ref[...] = mixed.astype(jnp.bfloat16)


def swap(x, axis, count, k):
    return lax.ppermute(x, axis, [(i, i ^ k) for i in range(count)])


def local(tokens, expert_ids, route_gates, up_weight, down_weight, *, expert_count, ctx_count, tensor_count):
    group_len, width = tokens.shape
    block_len = group_len // ctx_count
    capacity = block_len // 2
    per_expert = ctx_count * capacity
    rows = expert_count * per_expert
    hidden_local = up_weight.shape[1]
    chunk = hidden_local // tensor_count
    up_local = up_weight.reshape(up_weight.shape[1:])
    down_local = down_weight.reshape(down_weight.shape[1:])
    shape = jax.ShapeDtypeStruct
    bf16, f32 = jnp.bfloat16, jnp.float32

    outgoing = vmem_call(
        functools.partial(dispatch_body, block_len=block_len, capacity=capacity, per_expert=per_expert),
        (tokens, expert_ids),
        [shape((per_expert, width), bf16)] * expert_count,
        "dispatch",
        flops=AHEAD,
    )
    arrived = [outgoing[0]] + [swap(outgoing[k], "expert", expert_count, k) for k in range(1, expert_count)]

    flops = 2 * rows * width * chunk
    order = list(range(tensor_count - 1, 0, -1))
    parts = []
    for k in order:
        part = vmem_call(
            functools.partial(up_body, step=k, chunk=chunk), (*arrived, up_local), shape((rows, chunk), bf16),
            f"up{k}", flops,
        )
        parts.append(swap(part, "tensor", tensor_count, k))
    own = vmem_call(
        functools.partial(up_body, step=0, chunk=chunk), (*arrived, up_local), shape((rows, chunk), f32), "up0", flops
    )
    hidden = vmem_call(act_body, (own, *parts), shape((rows, chunk), bf16), "act")
    others = [(k, swap(hidden, "tensor", tensor_count, k)) for k in range(1, tensor_count)]
    total = vmem_call(
        functools.partial(down_body, step=0, chunk=chunk), (hidden, down_local), shape((rows, width), f32), "down0",
        flops,
    )
    for k, other in others[:-1]:
        total = vmem_call(
            functools.partial(down_body, step=k, chunk=chunk), (other, down_local, total), shape((rows, width), f32),
            f"down{k}", flops,
        )
    k, other = others[-1]
    leaving = vmem_call(
        functools.partial(last_body, step=k, chunk=chunk, ctx_count=ctx_count, capacity=capacity),
        (other, down_local, total),
        shape((expert_count * ctx_count, capacity, width), bf16),
        f"down{k}",
        flops,
    )
    back = lax.all_to_all(leaving, ("expert", "ctx"), 0, 0, tiled=True)
    return vmem_call(
        functools.partial(mix_body, block_len=block_len, capacity=capacity, ctx_count=ctx_count),
        (back, expert_ids, route_gates),
        shape((block_len, width), bf16),
        "mix",
    )


def solution(mesh):
    body = functools.partial(
        local,
        expert_count=mesh.shape["expert"],
        ctx_count=mesh.shape["ctx"],
        tensor_count=mesh.shape["tensor"],
    )
    in_specs = (
        P("expert", "tensor"),
        P("expert", None),
        P("expert", None),
        P("expert", "ctx", "tensor"),
        P("expert", "ctx", "tensor"),
    )
    out_specs = P(("expert", "ctx"), "tensor")
    return jax.shard_map(body, mesh=mesh, in_specs=in_specs, out_specs=out_specs, check_vma=False)
```

time: 107 us -> 46.6 us (0.44)
  blocking collectives: 34 us -> 0 us
  matrix products: 22.6 us -> 0 us
  starting transfers between devices: 3.27 us -> 16.8 us
  between operations: 13.5 us -> 0.13 us
  Pallas kernels: 0 us -> 11.5 us
  waiting for transfers between devices: 27.3 us -> 16.2 us
  other arithmetic: 2.87 us -> 0.01 us
    reduce_scatter x1 -> x0, waiting for transfers between devices: 23.5 us -> none  [local(): lax.psum_scatter(before_act, 'tensor', scatter_dimension=0, tiled=True)]
    dot_general x3 -> x0, matrix products: 22.6 us -> none  [the longest x1 12.8 us: local(): lax.dot_general(row_data, up_local, (((1,), (1,)), ((), ())), preferred_e...]
    all_gather x1 -> x0, blocking collectives: 15.3 us -> none  [local(): lax.all_gather(hidden, 'tensor', axis=0, tiled=True)]
    ppermute x0 -> x9, starting transfers between devices: none -> 13 us  [swap(): return lax.ppermute(x, axis, [(i, i ^ k) for i in range(count)])]
    pallas_call x0 -> x11, Pallas kernels: none -> 11.5 us  [vmem_call(): pl.pallas_call(body, in_specs=[VMEM] * len(args), out_specs=jax.tree.map(...]
    ppermute x0 -> x9, waiting for transfers between devices: none -> 11.5 us  [swap(): return lax.ppermute(x, axis, [(i, i ^ k) for i in range(count)])]
    psum x1 -> x0, blocking collectives: 10.5 us -> none  [local(): totals = lax.psum(by_block, 'ctx')]
    all_to_all x1 -> x0, blocking collectives: 8.33 us -> none  [local(): lax.all_to_all(outgoing, 'expert', split_axis=0, concat_axis=0, tiled=True)]
  transfers between devices with their start and end apart: 2 -> 10, of which waited for: 2 -> 6; matrix products, arithmetic and copies ran while one was open for 0% -> 0% of each run, Pallas kernels for 0% -> 15%
where the time goes in v1:
time: 46.6 us; the launch traced here: 46.3 us
  starting transfers between devices  16.8 us (36%)
  waiting for transfers between devices  16.2 us (35%)
  Pallas kernels  11.5 us (25%)
  local copies, waits for them, and re-layouts  1.71 us (4%)
    ppermute x9, starting transfers between devices, swap(): return lax.ppermute(x, axis, [(i, i ^ k) for i in range(count)])  13 us
    pallas_call x11, Pallas kernels, vmem_call(): pl.pallas_call(body, in_specs=[VMEM] * len(args), out_specs=jax.tree.map(...  11.5 us
    ppermute x9, waiting for transfers between devices, swap(): return lax.ppermute(x, axis, [(i, i ^ k) for i in range(count)])  11.5 us
    all_to_all x1, waiting for transfers between devices, local(): back = lax.all_to_all(leaving, ('expert', 'ctx'), 0, 0, tiled=True)  4.71 us
    all_to_all x1, starting transfers between devices, local(): back = lax.all_to_all(leaving, ('expert', 'ctx'), 0, 0, tiled=True)  3.73 us
    unnamed x18, local copies, waits for them, and re-layouts  1.71 us
  transfers between devices with their start and end apart: 10, of which 6 were waited for; matrix products, arithmetic and copies ran while one was open for 0% of the time, Pallas kernels for 15%

profile of v1, /device:TPU:0, one launch (start us, length us, event | category | flops | bytes accessed | tf_op | source)
XLA Modules:
  0.0 46.3 jit_solution(12026469214176095486)
XLA Ops:
  0.0 0.8 %copy.6.ids_ref = s32[16,2]{1,0:T(8,128)S(1)} copy(s32[16,2]{0,1:T(2,128)} %param.6) | data formatting | bytes 256 | tf_op args[1]
  0.8 0.0 copy-start.1
  0.8 0.8 %copy-done.1 = bf16[16,1536]{1,0:T(8,128)(2,1)S(1)} copy-done((bf16[16,1536]{1,0:T(8,128)(2,1)S(1)}, bf16[16,1536]{1,0:T(8,128)(2,1)}, u32[]{:S(2)}) %copy-start.1) | copy-done | bytes 49176
  1.6 0.0 copy-start
  1.6 0.4 dispatch.1
  1.9 0.6 %collective-permute-start = (bf16[8,1536]{1,0:T(8,128)(2,1)S(1)}, bf16[8,1536]{1,0:T(8,128)(2,1)S(1)}, u32[]{:S(2)}, u32[]{:S(2)}) collective-permute-start(bf16[8,1536]{1,0:T(8,128)(2,1)S(1)} %get-tuple-element.10), channel_id=1, source_target_pairs={{0,8},{8,0},{16,24},{24,16},{1,9},{9,1},{17,25},{25,17},{2,10},{10... | collective-permute-start | bytes 73736 | tf_op jit(solution)/shard_map/ppermute | solution.py:131
  2.5 2.6 %collective-permute-start.1 = (bf16[8,1536]{1,0:T(8,128)(2,1)S(1)}, bf16[8,1536]{1,0:T(8,128)(2,1)S(1)}, u32[]{:S(2)}, u32[]{:S(2)}) collective-permute-start(bf16[8,1536]{1,0:T(8,128)(2,1)S(1)} %get-tuple-element.11), channel_id=1, source_target_pairs={{0,16},{8,24},{16,0},{24,8},{1,17},{9,25},{17,1},{25,9},{2,18},{10... | collective-permute-start | bytes 73736 | tf_op jit(solution)/shard_map/ppermute | solution.py:131
  5.1 0.0 collective-permute-start.2
  5.1 0.0 collective-permute-done.refs_1_
  5.1 1.8 %collective-permute-done.1.refs_2_ = bf16[8,1536]{1,0:T(8,128)(2,1)S(1)} collective-permute-done((bf16[8,1536]{1,0:T(8,128)(2,1)S(1)}, bf16[8,1536]{1,0:T(8,128)(2,1)S(1)}, u32[]{:S(2)}, u32[]{:S(2)}) %collective-permute-start.1) | collective-permute-done | bytes 24608 | tf_op jit(solution)/shard_map/ppermute | solution.py:131
  6.9 1.4 %collective-permute-done.2.refs_3_ = bf16[8,1536]{1,0:T(8,128)(2,1)S(1)} collective-permute-done((bf16[8,1536]{1,0:T(8,128)(2,1)S(1)}, bf16[8,1536]{1,0:T(8,128)(2,1)S(1)}, u32[]{:S(2)}, u32[]{:S(2)}) %collective-permute-start.2) | collective-permute-done | bytes 24608 | tf_op jit(solution)/shard_map/ppermute | solution.py:131
  8.3 0.0 copy-done
  8.3 1.5 %up2.1 = bf16[32,1536]{1,0:T(8,128)(2,1)S(1)} custom-call(bf16[8,1536]{1,0:T(8,128)(2,1)S(1)} %get-tuple-element.9.refs_0_, bf16[8,1536]{1,0:T(8,128)(2,1)S(1)} %collective-permute-done.refs_1_, bf16[8,1536]{1,0:T(8,128)(2,1)S(1)} %collective-permute-done.1.refs_2_, bf16[8,1536]{1,0:T(8,128)(2,1)S(1)} %collective-permute-done.2.refs_3_, ...), custom_call_target="tpu_custom_call" | custom-call | flops 150994944 | tf_op jit(solution)/shard_map/up2/pallas_call | solution.py:20
  9.8 3.7 %collective-permute-start.4 = (bf16[32,1536]{1,0:T(8,128)(2,1)S(1)}, bf16[32,1536]{1,0:T(8,128)(2,1)S(1)}, u32[]{:S(2)}, u32[]{:S(2)}) collective-permute-start(bf16[32,1536]{1,0:T(8,128)(2,1)S(1)} %up2.1), channel_id=1, source_target_pairs={{0,2},{1,3},{2,0},{3,1},{4,6},{5,7},{6,4},{7,5},{8,10},{9,11},{10,... | collective-permute-start | bytes 294920 | tf_op jit(solution)/shard_map/ppermute | solution.py:131
  13.5 1.5 %up1.1 = bf16[32,1536]{1,0:T(8,128)(2,1)S(1)} custom-call(bf16[8,1536]{1,0:T(8,128)(2,1)S(1)} %get-tuple-element.9.refs_0_, bf16[8,1536]{1,0:T(8,128)(2,1)S(1)} %collective-permute-done.refs_1_, bf16[8,1536]{1,0:T(8,128)(2,1)S(1)} %collective-permute-done.1.refs_2_, bf16[8,1536]{1,0:T(8,128)(2,1)S(1)} %collective-permute-done.2.refs_3_, ...), custom_call_target="tpu_custom_call" | custom-call | flops 150994944 | tf_op jit(solution)/shard_map/up1/pallas_call | solution.py:20
  14.9 0.0 slice-start
  15.0 0.0 slice-start.1
  15.0 0.0 slice-start.2
  15.0 1.6 %collective-permute-start.5 = (bf16[32,1536]{1,0:T(8,128)(2,1)S(1)}, bf16[32,1536]{1,0:T(8,128)(2,1)S(1)}, u32[]{:S(2)}, u32[]{:S(2)}) collective-permute-start(bf16[32,1536]{1,0:T(8,128)(2,1)S(1)} %up1.1), channel_id=1, source_target_pairs={{0,1},{1,0},{2,3},{3,2},{4,5},{5,4},{6,7},{7,6},{8,9},{9,8},{10,11... | collective-permute-start | bytes 294920 | tf_op jit(solution)/shard_map/ppermute | solution.py:131
  16.6 1.5 %up3.1 = bf16[32,1536]{1,0:T(8,128)(2,1)S(1)} custom-call(bf16[8,1536]{1,0:T(8,128)(2,1)S(1)} %get-tuple-element.9.refs_0_, bf16[8,1536]{1,0:T(8,128)(2,1)S(1)} %collective-permute-done.refs_1_, bf16[8,1536]{1,0:T(8,128)(2,1)S(1)} %collective-permute-done.1.refs_2_, bf16[8,1536]{1,0:T(8,128)(2,1)S(1)} %collective-permute-done.2.refs_3_, ...), custom_call_target="tpu_custom_call" | custom-call | flops 150994944 | tf_op jit(solution)/shard_map/up3/pallas_call | solution.py:20
  18.1 0.0 slice-start.3
  18.1 0.0 slice-start.4
  18.1 0.1 collective-permute-start.3
  18.2 1.5 %up0.1.refs_0_ = f32[32,1536]{1,0:T(8,128)S(1)} custom-call(bf16[8,1536]{1,0:T(8,128)(2,1)S(1)} %get-tuple-element.9.refs_0_, bf16[8,1536]{1,0:T(8,128)(2,1)S(1)} %collective-permute-done.refs_1_, bf16[8,1536]{1,0:T(8,128)(2,1)S(1)} %collective-permute-done.1.refs_2_, bf16[8,1536]{1,0:T(8,128)(2,1)S(1)} %collective-permute-done.2.refs_3_, ...), custom_call_target="tpu_custom_call" | custom-call | flops 150994944 | tf_op jit(solution)/shard_map/up0/pallas_call | solution.py:20
  19.7 0.0 collective-permute-done.4.refs_2_
  19.7 0.5 collective-permute-done.5.refs_3_
  20.1 4.6 %collective-permute-done.3.refs_1_ = bf16[32,1536]{1,0:T(8,128)(2,1)S(1)} collective-permute-done((bf16[32,1536]{1,0:T(8,128)(2,1)S(1)}, bf16[32,1536]{1,0:T(8,128)(2,1)S(1)}, u32[]{:S(2)}, u32[]{:S(2)}) %collective-permute-start.3) | collective-permute-done | bytes 98336 | tf_op jit(solution)/shard_map/ppermute | solution.py:131
  24.7 0.1 act.1.refs_0_
  24.8 0.7 %collective-permute-start.8 = (bf16[32,1536]{1,0:T(8,128)(2,1)S(1)}, bf16[32,1536]{1,0:T(8,128)(2,1)S(1)}, u32[]{:S(2)}, u32[]{:S(2)}) collective-permute-start(bf16[32,1536]{1,0:T(8,128)(2,1)S(1)} %act.1.refs_0_), channel_id=1, source_target_pairs={{0,1},{1,0},{2,3},{3,2},{4,5},{5,4},{6,7},{7,6},{8,9},{9,8},{10,11... | collective-permute-start | bytes 294920 | tf_op jit(solution)/shard_map/ppermute | solution.py:131
  25.5 0.5 collective-permute-start.7
  25.9 3.3 %collective-permute-start.6 = (bf16[32,1536]{1,0:T(8,128)(2,1)S(1)}, bf16[32,1536]{1,0:T(8,128)(2,1)S(1)}, u32[]{:S(2)}, u32[]{:S(2)}) collective-permute-start(bf16[32,1536]{1,0:T(8,128)(2,1)S(1)} %act.1.refs_0_), channel_id=1, source_target_pairs={{0,3},{1,2},{2,1},{3,0},{4,7},{5,6},{6,5},{7,4},{8,11},{9,10},{10,... | collective-permute-start | bytes 294920 | tf_op jit(solution)/shard_map/ppermute | solution.py:131
  29.2 0.0 slice-done
  29.2 0.0 slice-done.1
  29.2 0.0 slice-done.2
  29.2 0.0 slice-done.3
  29.2 0.0 slice-done.4
  29.3 0.9 %down0.1.refs_2_ = f32[32,1536]{1,0:T(8,128)S(1)} custom-call(bf16[32,1536]{1,0:T(8,128)(2,1)S(1)} %act.1.refs_0_, bf16[6144,1536]{1,0:T(8,128)(2,1)S(1)} %bitcast.8), custom_call_target="tpu_custom_call" | custom-call | flops 150994944 | tf_op jit(solution)/shard_map/down0/pallas_call | solution.py:20
  30.2 0.0 collective-permute-done.8.refs_0_
  30.2 0.9 %down1.1.refs_2_ = f32[32,1536]{1,0:T(8,128)S(1)} custom-call(bf16[32,1536]{1,0:T(8,128)(2,1)S(1)} %collective-permute-done.8.refs_0_, bf16[6144,1536]{1,0:T(8,128)(2,1)S(1)} %bitcast.9, f32[32,1536]{1,0:T(8,128)S(1)} %down0.1.refs_2_), custom_call_target="tpu_custom_call" | custom-call | flops 150994944 | tf_op jit(solution)/shard_map/down1/pallas_call | solution.py:20
  31.1 3.2 %collective-permute-done.7.refs_0_ = bf16[32,1536]{1,0:T(8,128)(2,1)S(1)} collective-permute-done((bf16[32,1536]{1,0:T(8,128)(2,1)S(1)}, bf16[32,1536]{1,0:T(8,128)(2,1)S(1)}, u32[]{:S(2)}, u32[]{:S(2)}) %collective-permute-start.7) | collective-permute-done | bytes 98336 | tf_op jit(solution)/shard_map/ppermute | solution.py:131
  34.3 0.9 %down2.1.prior_ref = f32[32,1536]{1,0:T(8,128)S(1)} custom-call(bf16[32,1536]{1,0:T(8,128)(2,1)S(1)} %collective-permute-done.7.refs_0_, bf16[6144,1536]{1,0:T(8,128)(2,1)S(1)} %bitcast.10, f32[32,1536]{1,0:T(8,128)S(1)} %down1.1.refs_2_), custom_call_target="tpu_custom_call" | custom-call | flops 150994944 | tf_op jit(solution)/shard_map/down2/pallas_call | solution.py:20
  35.2 0.0 collective-permute-done.6.hidden_ref
  35.2 1.6 %down3.1 = bf16[8,4,1536]{2,1,0:T(4,128)(2,1)} custom-call(bf16[32,1536]{1,0:T(8,128)(2,1)S(1)} %collective-permute-done.6.hidden_ref, bf16[6144,1536]{1,0:T(8,128)(2,1)S(1)} %bitcast.11, f32[32,1536]{1,0:T(8,128)S(1)} %down2.1.prior_ref), custom_call_target="tpu_custom_call" | custom-call | flops 150994944 | tf_op jit(solution)/shard_map/down3/pallas_call | solution.py:20
  36.8 3.7 %all-to-all-start = ((bf16[8,4,1536]{2,1,0:T(4,128)(2,1)}), bf16[8,4,1536]{2,1,0:T(4,128)(2,1)S(1)}, u32[]{:S(2)}, u32[]{:S(2)}) async-start(bf16[8,4,1536]{2,1,0:T(4,128)(2,1)} %down3.1), calls=%async_computation | async-start | bytes 196608 | tf_op jit(solution)/shard_map/all_to_all | solution.py:187
  40.5 0.0 copy-done.2
  40.5 0.1 copy.8.gates_ref
  40.6 4.7 %all-to-all-done.back_ref = bf16[8,4,1536]{2,1,0:T(4,128)(2,1)S(1)} async-done(((bf16[8,4,1536]{2,1,0:T(4,128)(2,1)}), bf16[8,4,1536]{2,1,0:T(4,128)(2,1)S(1)}, u32[]{:S(2)}, u32[]{:S(2)}) %all-to-all-start) | async-done | bytes 98336 | tf_op jit(solution)/shard_map/all_to_all | solution.py:187
  45.3 1.0 %mix.1 = bf16[8,1536]{1,0:T(8,128)(2,1)} custom-call(bf16[8,4,1536]{2,1,0:T(4,128)(2,1)S(1)} %all-to-all-done.back_ref, s32[16,2]{1,0:T(8,128)S(1)} %copy.6.ids_ref, f32[16,2]{1,0:T(8,128)S(1)} %copy.8.gates_ref), custom_call_target="tpu_custom_call" | custom-call | tf_op jit(solution)/shard_map/mix/pallas_call | solution.py:20
  (2 shorter events, 0.0 us)
Async XLA Ops:
  0.8 0.8 %copy-start.1 = (bf16[16,1536]{1,0:T(8,128)(2,1)S(1)}, bf16[16,1536]{1,0:T(8,128)(2,1)}, u32[]{:S(2)}) copy-start(bf16[16,1536]{1,0:T(8,128)(2,1)} %tokens_ref.1) | copy-start | bytes 147460
  1.6 6.8 %copy-start = (bf16[1,6144,1536]{2,1,0:T(8,128)(2,1)S(1)}, bf16[1,6144,1536]{2,1,0:T(8,128)(2,1)}, u32[]{:S(2)}) copy-start(bf16[1,6144,1536]{2,1,0:T(8,128)(2,1)} %param.8) | copy-start | bytes 56623108
  1.9 3.2 %collective-permute-start = (bf16[8,1536]{1,0:T(8,128)(2,1)S(1)}, bf16[8,1536]{1,0:T(8,128)(2,1)S(1)}, u32[]{:S(2)}, u32[]{:S(2)}) collective-permute-start(bf16[8,1536]{1,0:T(8,128)(2,1)S(1)} %get-tuple-element.10), channel_id=1, source_target_pairs={{0,8},{8,0},{16,24},{24,16},{1,9},{9,1},{17,25},{25,17},{2,10},{10... | collective-permute-start | bytes 73736 | tf_op jit(solution)/shard_map/ppermute | solution.py:131
  2.5 4.4 %collective-permute-start.1 = (bf16[8,1536]{1,0:T(8,128)(2,1)S(1)}, bf16[8,1536]{1,0:T(8,128)(2,1)S(1)}, u32[]{:S(2)}, u32[]{:S(2)}) collective-permute-start(bf16[8,1536]{1,0:T(8,128)(2,1)S(1)} %get-tuple-element.11), channel_id=1, source_target_pairs={{0,16},{8,24},{16,0},{24,8},{1,17},{9,25},{17,1},{25,9},{2,18},{10... | collective-permute-start | bytes 73736 | tf_op jit(solution)/shard_map/ppermute | solution.py:131
  5.1 3.3 %collective-permute-start.2 = (bf16[8,1536]{1,0:T(8,128)(2,1)S(1)}, bf16[8,1536]{1,0:T(8,128)(2,1)S(1)}, u32[]{:S(2)}, u32[]{:S(2)}) collective-permute-start(bf16[8,1536]{1,0:T(8,128)(2,1)S(1)} %get-tuple-element.12), channel_id=1, source_target_pairs={{0,24},{8,16},{16,8},{24,0},{1,25},{9,17},{17,9},{25,1},{2,26},{10... | collective-permute-start | bytes 73736 | tf_op jit(solution)/shard_map/ppermute | solution.py:131
  9.8 9.9 %collective-permute-start.4 = (bf16[32,1536]{1,0:T(8,128)(2,1)S(1)}, bf16[32,1536]{1,0:T(8,128)(2,1)S(1)}, u32[]{:S(2)}, u32[]{:S(2)}) collective-permute-start(bf16[32,1536]{1,0:T(8,128)(2,1)S(1)} %up2.1), channel_id=1, source_target_pairs={{0,2},{1,3},{2,0},{3,1},{4,6},{5,7},{6,4},{7,5},{8,10},{9,11},{10,... | collective-permute-start | bytes 294920 | tf_op jit(solution)/shard_map/ppermute | solution.py:131
  14.9 14.3 %slice-start = ((s8[18874368]{0:T(1024)(128)(4,1)}), s8[4194304]{0:T(1024)(128)(4,1)S(1)}, s32[]{:S(2)}) async-start(s8[18874368]{0:T(1024)(128)(4,1)} %bitcast.6), calls=%async_computation.1 | async-start | bytes 8388608
  15.0 14.3 %slice-start.1 = ((s8[18874368]{0:T(1024)(128)(4,1)}), s8[4194304]{0:T(1024)(128)(4,1)S(1)}, s32[]{:S(2)}) async-start(s8[18874368]{0:T(1024)(128)(4,1)} %bitcast.6), calls=%async_computation.2 | async-start | bytes 8388608
  15.0 14.3 %slice-start.2 = ((s8[18874368]{0:T(1024)(128)(4,1)}), s8[4194304]{0:T(1024)(128)(4,1)S(1)}, s32[]{:S(2)}) async-start(s8[18874368]{0:T(1024)(128)(4,1)} %bitcast.6), calls=%async_computation.3 | async-start | bytes 8388608
  15.0 5.2 %collective-permute-start.5 = (bf16[32,1536]{1,0:T(8,128)(2,1)S(1)}, bf16[32,1536]{1,0:T(8,128)(2,1)S(1)}, u32[]{:S(2)}, u32[]{:S(2)}) collective-permute-start(bf16[32,1536]{1,0:T(8,128)(2,1)S(1)} %up1.1), channel_id=1, source_target_pairs={{0,1},{1,0},{2,3},{3,2},{4,5},{5,4},{6,7},{7,6},{8,9},{9,8},{10,11... | collective-permute-start | bytes 294920 | tf_op jit(solution)/shard_map/ppermute | solution.py:131
  18.1 11.1 %slice-start.3 = ((s8[18874368]{0:T(1024)(128)(4,1)}), s8[4194304]{0:T(1024)(128)(4,1)S(1)}, s32[]{:S(2)}) async-start(s8[18874368]{0:T(1024)(128)(4,1)} %bitcast.6), calls=%async_computation.4 | async-start | bytes 8388608
  18.1 11.1 %slice-start.4 = ((s8[18874368]{0:T(1024)(128)(4,1)}), s8[2097152]{0:T(1024)(128)(4,1)S(1)}, s32[]{:S(2)}) async-start(s8[18874368]{0:T(1024)(128)(4,1)} %bitcast.6), calls=%async_computation.5 | async-start | bytes 4194304
  18.1 6.6 %collective-permute-start.3 = (bf16[32,1536]{1,0:T(8,128)(2,1)S(1)}, bf16[32,1536]{1,0:T(8,128)(2,1)S(1)}, u32[]{:S(2)}, u32[]{:S(2)}) collective-permute-start(bf16[32,1536]{1,0:T(8,128)(2,1)S(1)} %up3.1), channel_id=1, source_target_pairs={{0,3},{1,2},{2,1},{3,0},{4,7},{5,6},{6,5},{7,4},{8,11},{9,10},{10,... | collective-permute-start | bytes 294920 | tf_op jit(solution)/shard_map/ppermute | solution.py:131
  24.8 5.4 %collective-permute-start.8 = (bf16[32,1536]{1,0:T(8,128)(2,1)S(1)}, bf16[32,1536]{1,0:T(8,128)(2,1)S(1)}, u32[]{:S(2)}, u32[]{:S(2)}) collective-permute-start(bf16[32,1536]{1,0:T(8,128)(2,1)S(1)} %act.1.refs_0_), channel_id=1, source_target_pairs={{0,1},{1,0},{2,3},{3,2},{4,5},{5,4},{6,7},{7,6},{8,9},{9,8},{10,11... | collective-permute-start | bytes 294920 | tf_op jit(solution)/shard_map/ppermute | solution.py:131
  25.5 8.8 %collective-permute-start.7 = (bf16[32,1536]{1,0:T(8,128)(2,1)S(1)}, bf16[32,1536]{1,0:T(8,128)(2,1)S(1)}, u32[]{:S(2)}, u32[]{:S(2)}) collective-permute-start(bf16[32,1536]{1,0:T(8,128)(2,1)S(1)} %act.1.refs_0_), channel_id=1, source_target_pairs={{0,2},{1,3},{2,0},{3,1},{4,6},{5,7},{6,4},{7,5},{8,10},{9,11},{10,... | collective-permute-start | bytes 294920 | tf_op jit(solution)/shard_map/ppermute | solution.py:131
  25.9 9.3 %collective-permute-start.6 = (bf16[32,1536]{1,0:T(8,128)(2,1)S(1)}, bf16[32,1536]{1,0:T(8,128)(2,1)S(1)}, u32[]{:S(2)}, u32[]{:S(2)}) collective-permute-start(bf16[32,1536]{1,0:T(8,128)(2,1)S(1)} %act.1.refs_0_), channel_id=1, source_target_pairs={{0,3},{1,2},{2,1},{3,0},{4,7},{5,6},{6,5},{7,4},{8,11},{9,10},{10,... | collective-permute-start | bytes 294920 | tf_op jit(solution)/shard_map/ppermute | solution.py:131
  31.1 9.5 %copy-start.2 = (f32[16,2]{0,1:T(2,128)S(1)}, f32[16,2]{0,1:T(2,128)}, u32[]{:S(2)}) copy-start(f32[16,2]{0,1:T(2,128)} %param.7) | copy-start | bytes 388
  36.8 8.5 %all-to-all-start = ((bf16[8,4,1536]{2,1,0:T(4,128)(2,1)}), bf16[8,4,1536]{2,1,0:T(4,128)(2,1)S(1)}, u32[]{:S(2)}, u32[]{:S(2)}) async-start(bf16[8,4,1536]{2,1,0:T(4,128)(2,1)} %down3.1), calls=%async_computation | async-start | bytes 196608 | tf_op jit(solution)/shard_map/all_to_all | solution.py:187

commit v2 on v1

--- a/solution.py
+++ b/solution.py
@@ -28,42 +28,71 @@
     )(*args)
 
 
-def named_before(ids, expert_row, block_len):
-    count = ids.shape[0]
-    first = ids[:, 0:1] == expert_row
-    second = ids[:, 1:2] == expert_row
-    names = jnp.where(first | second, 1.0, 0.0)
-    row = lax.broadcasted_iota(jnp.int32, (count, count), 0)
-    col = lax.broadcasted_iota(jnp.int32, (count, count), 1)
-    shift = shift_of(block_len)
-    earlier = (col < row) & (lax.shift_right_logical(row, shift) == lax.shift_right_logical(col, shift))
+def lane_iota(shape):
+    return lax.broadcasted_iota(jnp.int32, shape, 1)
+
+
+def row_iota(shape):
+    return lax.broadcasted_iota(jnp.int32, shape, 0)
+
+
+def ones_where(mask, dtype):
+    return jnp.where(mask, 1.0, 0.0).astype(dtype)
+
+
+def dispatch_body(tokens_hbm, ids_hbm, gates_hbm, *refs, block_len, capacity, per_expert, expert_count):
+    *out_refs, pick_ref, gate_ref, tokens_ref, ids_ref, gates_ref, sem = refs
+    copies = [
+        pltpu.make_async_copy(src, dst, sem.at[i])
+        for i, (src, dst) in enumerate(((ids_hbm, ids_ref), (gates_hbm, gates_ref), (tokens_hbm, tokens_ref)))
+    ]
+    for copy in copies:
+        copy.start()
+    copies[0].wait()
+    first, second = ids_ref[0:1, :], ids_ref[1:2, :]
+    group_len = first.shape[1]
+    block_shift, cap_shift = shift_of(block_len), shift_of(capacity)
+    count = per_expert * expert_count
+    row = row_iota((count, 1))
+    expert = lax.axis_index("expert") ^ lax.shift_right_logical(row, shift_of(per_expert))
+    names = (first == expert) | (second == expert)
+    earlier_token, token = row_iota((group_len, group_len)), lane_iota((group_len, group_len))
+    before = (earlier_token < token) & (
+        lax.shift_right_logical(earlier_token, block_shift) == lax.shift_right_logical(token, block_shift)
+    )
     slot = jnp.dot(
-        jnp.where(earlier, 1.0, 0.0).astype(jnp.bfloat16),
-        names.astype(jnp.bfloat16),
-        preferred_element_type=jnp.float32,
-    )
-    return first, second, names, slot
-
-
-def dispatch_body(tokens_ref, ids_ref, *out_refs, block_len, capacity, per_expert):
-    ids = ids_ref[...]
-    group_len = ids.shape[0]
-    lanes = per_expert * len(out_refs)
-    lane = lax.broadcasted_iota(jnp.int32, (1, lanes), 1)
-    expert_row = lax.axis_index("expert") ^ lax.shift_right_logical(lane, shift_of(per_expert))
-    _, _, names, slot = named_before(ids, expert_row, block_len)
-    want_slot = (lane & (capacity - 1)).astype(jnp.float32)
-    want_block = lax.shift_right_logical(lane, shift_of(capacity)) & (per_expert // capacity - 1)
-    token = lax.broadcasted_iota(jnp.int32, (group_len, lanes), 0)
-    hit = (names > 0) & (slot == want_slot) & (lax.shift_right_logical(token, shift_of(block_len)) == want_block)
-    rows = lax.dot_general(
-        jnp.where(hit, 1.0, 0.0).astype(jnp.bfloat16),
-        tokens_ref[...],
-        (((0,), (0,)), ((), ())),
-        preferred_element_type=jnp.float32,
+        ones_where(names, jnp.bfloat16), ones_where(before, jnp.bfloat16), preferred_element_type=jnp.float32
+    )
+    block_of_row = lax.shift_right_logical(row, cap_shift) & (per_expert // capacity - 1)
+    block_of_token = lax.shift_right_logical(lane_iota((1, group_len)), block_shift)
+    hit = names & (slot == (row & (capacity - 1)).astype(jnp.float32)) & (block_of_row == block_of_token)
+    copies[2].wait()
+    rows = jnp.dot(
+        ones_where(hit, jnp.bfloat16), tokens_ref[...], preferred_element_type=jnp.float32
     ).astype(jnp.bfloat16)
     for k, ref in enumerate(out_refs):
         ref[...] = rows[k * per_expert:(k + 1) * per_expert]
+
+    copies[1].wait()
+    own_start = lax.axis_index("ctx") * block_len
+    own = row_iota((block_len, group_len)) + own_start
+    lane = lane_iota((block_len, group_len))
+    here = ones_where(own == lane, jnp.float32)
+    ahead = (lane < own) & (lane >= own_start)
+    halves = pick_ref.shape[0] // (2 * block_len)
+    wide = lane_iota((block_len, pick_ref.shape[1]))
+    for choice, named in enumerate((first, second)):
+        chosen = jnp.sum(here * named.astype(jnp.float32), axis=1, keepdims=True).astype(jnp.int32)
+        again = ahead & ((first == chosen) | (second == chosen))
+        own_slot = jnp.sum(ones_where(again, jnp.float32), axis=1, keepdims=True).astype(jnp.int32)
+        for half in range(halves):
+            at = (half * 2 + choice) * block_len
+            source = chosen * (halves * capacity) + half * capacity + own_slot
+            pick_ref[at:at + block_len, :] = ones_where(wide == source, jnp.bfloat16)
+        gate = jnp.sum(here * gates_ref[choice:choice + 1, :], axis=1, keepdims=True)
+        gate_ref[choice * block_len:(choice + 1) * block_len, :] = jnp.broadcast_to(
+            gate, (block_len, gate_ref.shape[1])
+        )
 
 
 def up_body(*refs, step, chunk):
@@ -98,33 +127,36 @@
         hidden_ref[...], down_ref[pl.ds(start, chunk), :], preferred_element_type=jnp.float32
     )
     mine = lax.axis_index("expert")
+    width = out_ref.shape[1]
+    halves = total.shape[1] // width
     for piece in range(total.shape[0] // capacity):
         k, b = piece // ctx_count, piece % ctx_count
-        dest = (mine ^ k) * ctx_count + b
-        out_ref[dest] = total[piece * capacity:(piece + 1) * capacity].astype(out_ref.dtype)
-
-
-def mix_body(back_ref, ids_ref, gates_ref, out_ref, *, block_len, capacity, ctx_count):
-    lanes_all = back_ref.shape[0]
-    expert_count = lanes_all // ctx_count
+        dest = pl.multiple_of(((mine ^ k) * ctx_count + b) * (halves * capacity), halves * capacity)
+        rows = total[piece * capacity:(piece + 1) * capacity]
+        cut = jnp.concatenate([rows[:, h * width:(h + 1) * width] for h in range(halves)], axis=0)
+        out_ref[pl.ds(dest, halves * capacity), :] = cut.astype(out_ref.dtype)
+
+
+def mix_body(back_ref, pick_ref, gate_ref, out_ref, *, ctx_count, piece_len):
+    width = back_ref.shape[1]
     picked = []
-    for e in range(expert_count):
-        total = back_ref[e * ctx_count].astype(jnp.float32)
+    for e in range(back_ref.shape[0] // (piece_len * ctx_count)):
+        at = e * ctx_count * piece_len
+        total = back_ref[at:at + piece_len].astype(jnp.float32)
         for c in range(1, ctx_count):
-            total = total + back_ref[e * ctx_count + c].astype(jnp.float32)
+            total = total + back_ref[at + c * piece_len:at + (c + 1) * piece_len].astype(jnp.float32)
         picked.append(total)
     rows = jnp.concatenate(picked, axis=0).astype(jnp.bfloat16)
-    start = pl.multiple_of(lax.axis_index("ctx") * block_len, block_len)
-    ids = ids_ref[pl.ds(start, block_len), :]
-    gates = gates_ref[pl.ds(start, block_len), :]
-    lane = lax.broadcasted_iota(jnp.int32, (1, expert_count * capacity), 1)
-    first, second, _, slot = named_before(ids, lax.shift_right_logical(lane, shift_of(capacity)), block_len)
-    here = slot == (lane & (capacity - 1)).astype(jnp.float32)
-    mixed = 0.0
-    for which, gate in ((first, gates[:, 0:1]), (second, gates[:, 1:2])):
-        pick = jnp.where(which & here, 1.0, 0.0).astype(jnp.bfloat16)
-        mixed = mixed + gate * jnp.dot(pick, rows, preferred_element_type=jnp.float32)
-    out_ref[...] = mixed.astype(jnp.bfloat16)
+    chosen = jnp.dot(pick_ref[...], rows, preferred_element_type=jnp.float32)
+    block_len = out_ref.shape[0]
+    gates = gate_ref[...]
+    for half in range(out_ref.shape[1] // width):
+        at = half * 2 * block_len
+        mixed = (
+            gates[:block_len, 0:1] * chosen[at:at + block_len]
+            + gates[block_len:, 0:1] * chosen[at + block_len:at + 2 * block_len]
+        )
+        out_ref[:, half * width:(half + 1) * width] = mixed.astype(jnp.bfloat16)
 
 
 def swap(x, axis, count, k):
@@ -144,13 +176,26 @@
     shape = jax.ShapeDtypeStruct
     bf16, f32 = jnp.bfloat16, jnp.float32
 
-    outgoing = vmem_call(
-        functools.partial(dispatch_body, block_len=block_len, capacity=capacity, per_expert=per_expert),
-        (tokens, expert_ids),
-        [shape((per_expert, width), bf16)] * expert_count,
-        "dispatch",
-        flops=AHEAD,
-    )
+    halves = max(1, 8 // capacity)
+    piece_len = halves * capacity
+    *outgoing, pick, gate = pl.pallas_call(
+        functools.partial(
+            dispatch_body, block_len=block_len, capacity=capacity, per_expert=per_expert, expert_count=expert_count
+        ),
+        in_specs=[pl.BlockSpec(memory_space=pltpu.HBM)] * 3,
+        out_specs=[VMEM] * (expert_count + 2),
+        out_shape=[shape((per_expert, width), bf16)] * expert_count
+        + [shape((halves * 2 * block_len, expert_count * piece_len), bf16), shape((2 * block_len, 128), f32)],
+        scratch_shapes=[
+            pltpu.VMEM((group_len, width), bf16),
+            pltpu.VMEM((2, group_len), jnp.int32),
+            pltpu.VMEM((2, group_len), f32),
+            pltpu.SemaphoreType.DMA((3,)),
+        ],
+        name="dispatch",
+        cost_estimate=pl.CostEstimate(flops=AHEAD, transcendentals=0, bytes_accessed=0),
+        compiler_params=pltpu.CompilerParams(vmem_limit_bytes=4 * MIB),
+    )(*[pltpu.with_memory_space_constraint(x, pltpu.HBM) for x in (tokens, expert_ids.T, route_gates.T)])
     arrived = [outgoing[0]] + [swap(outgoing[k], "expert", expert_count, k) for k in range(1, expert_count)]
 
     flops = 2 * rows * width * chunk
@@ -180,14 +225,14 @@
     leaving = vmem_call(
         functools.partial(last_body, step=k, chunk=chunk, ctx_count=ctx_count, capacity=capacity),
         (other, down_local, total),
-        shape((expert_count * ctx_count, capacity, width), bf16),
+        shape((expert_count * ctx_count * piece_len, width // halves), bf16),
         f"down{k}",
         flops,
     )
     back = lax.all_to_all(leaving, ("expert", "ctx"), 0, 0, tiled=True)
     return vmem_call(
-        functools.partial(mix_body, block_len=block_len, capacity=capacity, ctx_count=ctx_count),
-        (back, expert_ids, route_gates),
+        functools.partial(mix_body, ctx_count=ctx_count, piece_len=piece_len),
+        (back, pick, gate),
         shape((block_len, width), bf16),
         "mix",
     )

time: 46.6 us -> 43.9 us (0.942)
  blocking collectives: 0 us -> 8.09 us
  starting transfers between devices: 16.8 us -> 12.1 us
  waiting for transfers between devices: 16.2 us -> 11.7 us
  local copies, waits for them, and re-layouts: 1.71 us -> 0.07 us
    all_to_all x0 -> x1, blocking collectives: none -> 8.09 us  [local(): back = lax.all_to_all(leaving, ('expert', 'ctx'), 0, 0, tiled=True)]
    all_to_all x1 -> x0, waiting for transfers between devices: 4.71 us -> none  [local(): back = lax.all_to_all(leaving, ('expert', 'ctx'), 0, 0, tiled=True)]
    all_to_all x1 -> x0, starting transfers between devices: 3.73 us -> none  [local(): back = lax.all_to_all(leaving, ('expert', 'ctx'), 0, 0, tiled=True)]
    unnamed x18 -> x12, local copies, waits for them, and re-layouts: 1.71 us -> 0.07 us
    pallas_call x0 -> x1, Pallas kernels: none -> 1.33 us  [local(): pl.pallas_call(functools.partial(dispatch_body, block_len=block_len, capa...]
    pallas_call x11 -> x10, Pallas kernels: 11.5 us -> 10.3 us  [vmem_call(): pl.pallas_call(body, in_specs=[VMEM] * len(args), out_specs=jax.tree.map(...]
    ppermute x9, starting transfers between devices: 13 us -> 12.1 us  [swap(): return lax.ppermute(x, axis, [(i, i ^ k) for i in range(count)])]
  transfers between devices with their start and end apart: 10 -> 9, of which waited for: 6 -> 5; matrix products, arithmetic and copies ran while one was open for 0% -> 0% of each run, Pallas kernels for 15% -> 16%
where the time goes in v2:
time: 43.9 us; the launch traced here: 43.7 us
  starting transfers between devices  12.1 us (28%)
  waiting for transfers between devices  11.7 us (27%)
  Pallas kernels  11.6 us (26%)
  blocking collectives  8.09 us (18%)
    ppermute x9, starting transfers between devices, swap(): return lax.ppermute(x, axis, [(i, i ^ k) for i in range(count)])  12.1 us
    ppermute x9, waiting for transfers between devices, swap(): return lax.ppermute(x, axis, [(i, i ^ k) for i in range(count)])  11.7 us
    pallas_call x10, Pallas kernels, vmem_call(): pl.pallas_call(body, in_specs=[VMEM] * len(args), out_specs=jax.tree.map(...  10.3 us
    all_to_all x1, blocking collectives, local(): back = lax.all_to_all(leaving, ('expert', 'ctx'), 0, 0, tiled=True)  8.09 us
    pallas_call x1, Pallas kernels, local(): pl.pallas_call(functools.partial(dispatch_body, block_len=block_len, capa...  1.33 us
  transfers between devices with their start and end apart: 9, of which 5 were waited for; matrix products, arithmetic and copies ran while one was open for 0% of the time, Pallas kernels for 16%

profile of v2, /device:TPU:0, one launch (start us, length us, event | category | flops | bytes accessed | tf_op | source)
XLA Modules:
  0.0 43.7 jit_solution(8673965658610100705)
XLA Ops:
  0.0 0.0 copy-start
  0.0 1.3 %dispatch.1 = (bf16[8,1536]{1,0:T(8,128)(2,1)S(1)}, bf16[8,1536]{1,0:T(8,128)(2,1)S(1)}, bf16[8,1536]{1,0:T(8,128)(2,1)S(1)}, bf16[8,1536]{1,0:T(8,128)(2,1)S(1)...) custom-call(bf16[16,1536]{1,0:T(8,128)(2,1)} %tokens_hbm.1, s32[2,16]{1,0:T(2,128)} %bitcast.18, f32[2,16]{1,0:T(2,128)} %bitcast.19), custom_call_target="tpu_custom_call" | custom-call | flops 17179869184 | tf_op jit(solution)/shard_map/dispatch/pallas_call | solution.py:181
  1.3 0.6 %collective-permute-start = (bf16[8,1536]{1,0:T(8,128)(2,1)S(1)}, bf16[8,1536]{1,0:T(8,128)(2,1)S(1)}, u32[]{:S(2)}, u32[]{:S(2)}) collective-permute-start(bf16[8,1536]{1,0:T(8,128)(2,1)S(1)} %get-tuple-element.12), channel_id=1, source_target_pairs={{0,8},{8,0},{16,24},{24,16},{1,9},{9,1},{17,25},{25,17},{2,10},{10... | collective-permute-start | bytes 73736 | tf_op jit(solution)/shard_map/ppermute | solution.py:163
  1.9 2.5 %collective-permute-start.1 = (bf16[8,1536]{1,0:T(8,128)(2,1)S(1)}, bf16[8,1536]{1,0:T(8,128)(2,1)S(1)}, u32[]{:S(2)}, u32[]{:S(2)}) collective-permute-start(bf16[8,1536]{1,0:T(8,128)(2,1)S(1)} %get-tuple-element.13), channel_id=1, source_target_pairs={{0,16},{8,24},{16,0},{24,8},{1,17},{9,25},{17,1},{25,9},{2,18},{10... | collective-permute-start | bytes 73736 | tf_op jit(solution)/shard_map/ppermute | solution.py:163
  4.4 0.0 collective-permute-start.2
  4.5 0.0 collective-permute-done.refs_1_
  4.5 1.8 %collective-permute-done.1.refs_2_ = bf16[8,1536]{1,0:T(8,128)(2,1)S(1)} collective-permute-done((bf16[8,1536]{1,0:T(8,128)(2,1)S(1)}, bf16[8,1536]{1,0:T(8,128)(2,1)S(1)}, u32[]{:S(2)}, u32[]{:S(2)}) %collective-permute-start.1) | collective-permute-done | bytes 24608 | tf_op jit(solution)/shard_map/ppermute | solution.py:163
  6.3 1.4 %collective-permute-done.2.refs_3_ = bf16[8,1536]{1,0:T(8,128)(2,1)S(1)} collective-permute-done((bf16[8,1536]{1,0:T(8,128)(2,1)S(1)}, bf16[8,1536]{1,0:T(8,128)(2,1)S(1)}, u32[]{:S(2)}, u32[]{:S(2)}) %collective-permute-start.2) | collective-permute-done | bytes 24608 | tf_op jit(solution)/shard_map/ppermute | solution.py:163
  7.7 0.0 copy-done
  7.7 1.5 %up2.1 = bf16[32,1536]{1,0:T(8,128)(2,1)S(1)} custom-call(bf16[8,1536]{1,0:T(8,128)(2,1)S(1)} %get-tuple-element.11.refs_0_, bf16[8,1536]{1,0:T(8,128)(2,1)S(1)} %collective-permute-done.refs_1_, bf16[8,1536]{1,0:T(8,128)(2,1)S(1)} %collective-permute-done.1.refs_2_, bf16[8,1536]{1,0:T(8,128)(2,1)S(1)} %collective-permute-done.2.refs_3_, ...), custom_call_target="tpu_custom_call" | custom-call | flops 150994944 | tf_op jit(solution)/shard_map/up2/pallas_call | solution.py:20
  9.2 2.8 %collective-permute-start.4 = (bf16[32,1536]{1,0:T(8,128)(2,1)S(1)}, bf16[32,1536]{1,0:T(8,128)(2,1)S(1)}, u32[]{:S(2)}, u32[]{:S(2)}) collective-permute-start(bf16[32,1536]{1,0:T(8,128)(2,1)S(1)} %up2.1), channel_id=1, source_target_pairs={{0,2},{1,3},{2,0},{3,1},{4,6},{5,7},{6,4},{7,5},{8,10},{9,11},{10,... | collective-permute-start | bytes 294920 | tf_op jit(solution)/shard_map/ppermute | solution.py:163
  12.0 1.5 %up1.1 = bf16[32,1536]{1,0:T(8,128)(2,1)S(1)} custom-call(bf16[8,1536]{1,0:T(8,128)(2,1)S(1)} %get-tuple-element.11.refs_0_, bf16[8,1536]{1,0:T(8,128)(2,1)S(1)} %collective-permute-done.refs_1_, bf16[8,1536]{1,0:T(8,128)(2,1)S(1)} %collective-permute-done.1.refs_2_, bf16[8,1536]{1,0:T(8,128)(2,1)S(1)} %collective-permute-done.2.refs_3_, ...), custom_call_target="tpu_custom_call" | custom-call | flops 150994944 | tf_op jit(solution)/shard_map/up1/pallas_call | solution.py:20
  13.4 0.0 slice-start
  13.5 0.0 slice-start.1
  13.5 0.0 slice-start.2
  13.5 1.6 %collective-permute-start.5 = (bf16[32,1536]{1,0:T(8,128)(2,1)S(1)}, bf16[32,1536]{1,0:T(8,128)(2,1)S(1)}, u32[]{:S(2)}, u32[]{:S(2)}) collective-permute-start(bf16[32,1536]{1,0:T(8,128)(2,1)S(1)} %up1.1), channel_id=1, source_target_pairs={{0,1},{1,0},{2,3},{3,2},{4,5},{5,4},{6,7},{7,6},{8,9},{9,8},{10,11... | collective-permute-start | bytes 294920 | tf_op jit(solution)/shard_map/ppermute | solution.py:163
  15.1 1.5 %up3.1 = bf16[32,1536]{1,0:T(8,128)(2,1)S(1)} custom-call(bf16[8,1536]{1,0:T(8,128)(2,1)S(1)} %get-tuple-element.11.refs_0_, bf16[8,1536]{1,0:T(8,128)(2,1)S(1)} %collective-permute-done.refs_1_, bf16[8,1536]{1,0:T(8,128)(2,1)S(1)} %collective-permute-done.1.refs_2_, bf16[8,1536]{1,0:T(8,128)(2,1)S(1)} %collective-permute-done.2.refs_3_, ...), custom_call_target="tpu_custom_call" | custom-call | flops 150994944 | tf_op jit(solution)/shard_map/up3/pallas_call | solution.py:20
  16.6 0.0 slice-start.3
  16.6 0.0 slice-start.4
  16.6 0.1 collective-permute-start.3
  16.7 1.5 %up0.1.refs_0_ = f32[32,1536]{1,0:T(8,128)S(1)} custom-call(bf16[8,1536]{1,0:T(8,128)(2,1)S(1)} %get-tuple-element.11.refs_0_, bf16[8,1536]{1,0:T(8,128)(2,1)S(1)} %collective-permute-done.refs_1_, bf16[8,1536]{1,0:T(8,128)(2,1)S(1)} %collective-permute-done.1.refs_2_, bf16[8,1536]{1,0:T(8,128)(2,1)S(1)} %collective-permute-done.2.refs_3_, ...), custom_call_target="tpu_custom_call" | custom-call | flops 150994944 | tf_op jit(solution)/shard_map/up0/pallas_call | solution.py:20
  18.2 0.0 collective-permute-done.4.refs_2_
  18.2 0.7 %collective-permute-done.5.refs_3_ = bf16[32,1536]{1,0:T(8,128)(2,1)S(1)} collective-permute-done((bf16[32,1536]{1,0:T(8,128)(2,1)S(1)}, bf16[32,1536]{1,0:T(8,128)(2,1)S(1)}, u32[]{:S(2)}, u32[]{:S(2)}) %collective-permute-start.5) | collective-permute-done | bytes 98336 | tf_op jit(solution)/shard_map/ppermute | solution.py:163
  18.9 4.2 %collective-permute-done.3.refs_1_ = bf16[32,1536]{1,0:T(8,128)(2,1)S(1)} collective-permute-done((bf16[32,1536]{1,0:T(8,128)(2,1)S(1)}, bf16[32,1536]{1,0:T(8,128)(2,1)S(1)}, u32[]{:S(2)}, u32[]{:S(2)}) %collective-permute-start.3) | collective-permute-done | bytes 98336 | tf_op jit(solution)/shard_map/ppermute | solution.py:163
  23.1 0.1 act.1.refs_0_
  23.2 0.8 %collective-permute-start.8 = (bf16[32,1536]{1,0:T(8,128)(2,1)S(1)}, bf16[32,1536]{1,0:T(8,128)(2,1)S(1)}, u32[]{:S(2)}, u32[]{:S(2)}) collective-permute-start(bf16[32,1536]{1,0:T(8,128)(2,1)S(1)} %act.1.refs_0_), channel_id=1, source_target_pairs={{0,1},{1,0},{2,3},{3,2},{4,5},{5,4},{6,7},{7,6},{8,9},{9,8},{10,11... | collective-permute-start | bytes 294920 | tf_op jit(solution)/shard_map/ppermute | solution.py:163
  24.0 0.5 %collective-permute-start.7 = (bf16[32,1536]{1,0:T(8,128)(2,1)S(1)}, bf16[32,1536]{1,0:T(8,128)(2,1)S(1)}, u32[]{:S(2)}, u32[]{:S(2)}) collective-permute-start(bf16[32,1536]{1,0:T(8,128)(2,1)S(1)} %act.1.refs_0_), channel_id=1, source_target_pairs={{0,2},{1,3},{2,0},{3,1},{4,6},{5,7},{6,4},{7,5},{8,10},{9,11},{10,... | collective-permute-start | bytes 294920 | tf_op jit(solution)/shard_map/ppermute | solution.py:163
  24.4 3.2 %collective-permute-start.6 = (bf16[32,1536]{1,0:T(8,128)(2,1)S(1)}, bf16[32,1536]{1,0:T(8,128)(2,1)S(1)}, u32[]{:S(2)}, u32[]{:S(2)}) collective-permute-start(bf16[32,1536]{1,0:T(8,128)(2,1)S(1)} %act.1.refs_0_), channel_id=1, source_target_pairs={{0,3},{1,2},{2,1},{3,0},{4,7},{5,6},{6,5},{7,4},{8,11},{9,10},{10,... | collective-permute-start | bytes 294920 | tf_op jit(solution)/shard_map/ppermute | solution.py:163
  27.6 0.0 slice-done
  27.6 0.0 slice-done.1
  27.6 0.0 slice-done.2
  27.6 0.0 slice-done.3
  27.6 0.0 slice-done.4
  27.7 0.9 %down0.1.refs_2_ = f32[32,1536]{1,0:T(8,128)S(1)} custom-call(bf16[32,1536]{1,0:T(8,128)(2,1)S(1)} %act.1.refs_0_, bf16[6144,1536]{1,0:T(8,128)(2,1)S(1)} %bitcast.12), custom_call_target="tpu_custom_call" | custom-call | flops 150994944 | tf_op jit(solution)/shard_map/down0/pallas_call | solution.py:20
  28.6 0.0 collective-permute-done.8.refs_0_
  28.6 0.9 %down1.1.refs_2_ = f32[32,1536]{1,0:T(8,128)S(1)} custom-call(bf16[32,1536]{1,0:T(8,128)(2,1)S(1)} %collective-permute-done.8.refs_0_, bf16[6144,1536]{1,0:T(8,128)(2,1)S(1)} %bitcast.13, f32[32,1536]{1,0:T(8,128)S(1)} %down0.1.refs_2_), custom_call_target="tpu_custom_call" | custom-call | flops 150994944 | tf_op jit(solution)/shard_map/down1/pallas_call | solution.py:20
  29.5 3.6 %collective-permute-done.7.refs_0_ = bf16[32,1536]{1,0:T(8,128)(2,1)S(1)} collective-permute-done((bf16[32,1536]{1,0:T(8,128)(2,1)S(1)}, bf16[32,1536]{1,0:T(8,128)(2,1)S(1)}, u32[]{:S(2)}, u32[]{:S(2)}) %collective-permute-start.7) | collective-permute-done | bytes 98336 | tf_op jit(solution)/shard_map/ppermute | solution.py:163
  33.1 0.9 %down2.1.prior_ref = f32[32,1536]{1,0:T(8,128)S(1)} custom-call(bf16[32,1536]{1,0:T(8,128)(2,1)S(1)} %collective-permute-done.7.refs_0_, bf16[6144,1536]{1,0:T(8,128)(2,1)S(1)} %bitcast.14, f32[32,1536]{1,0:T(8,128)S(1)} %down1.1.refs_2_), custom_call_target="tpu_custom_call" | custom-call | flops 150994944 | tf_op jit(solution)/shard_map/down2/pallas_call | solution.py:20
  33.9 0.0 collective-permute-done.6.hidden_ref
  34.0 0.9 %down3.1 = bf16[64,768]{1,0:T(8,128)(2,1)S(1)} custom-call(bf16[32,1536]{1,0:T(8,128)(2,1)S(1)} %collective-permute-done.6.hidden_ref, bf16[6144,1536]{1,0:T(8,128)(2,1)S(1)} %bitcast.15, f32[32,1536]{1,0:T(8,128)S(1)} %down2.1.prior_ref), custom_call_target="tpu_custom_call" | custom-call | flops 150994944 | tf_op jit(solution)/shard_map/down3/pallas_call | solution.py:20
  34.9 8.1 %all_to_all.11 = bf16[8,8,768]{2,1,0:T(8,128)(2,1)S(1)} all-to-all(bf16[8,8,768]{2,1,0:T(8,128)(2,1)S(1)} %bitcast.16), channel_id=1, replica_groups=mesh['expert'=4,'ctx'=2,'tensor'=4] {'expert','ctx'}, dimensions={0} | all-to-all | bytes 196608 | tf_op jit(solution)/shard_map/all_to_all | solution.py:232
  43.0 0.7 %mix.1 = bf16[8,1536]{1,0:T(8,128)(2,1)} custom-call(bf16[64,768]{1,0:T(8,128)(2,1)S(1)} %bitcast.17, bf16[32,32]{1,0:T(8,128)(2,1)S(1)} %get-tuple-element.15.pick_ref, f32[16,128]{1,0:T(8,128)S(1)} %get-tuple-element.16.gate_ref), custom_call_target="tpu_custom_call" | custom-call | tf_op jit(solution)/shard_map/mix/pallas_call | solution.py:20
  (1 shorter events, 0.0 us)
Async XLA Ops:
  0.0 7.7 %copy-start = (bf16[1,6144,1536]{2,1,0:T(8,128)(2,1)S(1)}, bf16[1,6144,1536]{2,1,0:T(8,128)(2,1)}, u32[]{:S(2)}) copy-start(bf16[1,6144,1536]{2,1,0:T(8,128)(2,1)} %param.8) | copy-start | bytes 56623108
  1.3 3.2 %collective-permute-start = (bf16[8,1536]{1,0:T(8,128)(2,1)S(1)}, bf16[8,1536]{1,0:T(8,128)(2,1)S(1)}, u32[]{:S(2)}, u32[]{:S(2)}) collective-permute-start(bf16[8,1536]{1,0:T(8,128)(2,1)S(1)} %get-tuple-element.12), channel_id=1, source_target_pairs={{0,8},{8,0},{16,24},{24,16},{1,9},{9,1},{17,25},{25,17},{2,10},{10... | collective-permute-start | bytes 73736 | tf_op jit(solution)/shard_map/ppermute | solution.py:163
  1.9 4.4 %collective-permute-start.1 = (bf16[8,1536]{1,0:T(8,128)(2,1)S(1)}, bf16[8,1536]{1,0:T(8,128)(2,1)S(1)}, u32[]{:S(2)}, u32[]{:S(2)}) collective-permute-start(bf16[8,1536]{1,0:T(8,128)(2,1)S(1)} %get-tuple-element.13), channel_id=1, source_target_pairs={{0,16},{8,24},{16,0},{24,8},{1,17},{9,25},{17,1},{25,9},{2,18},{10... | collective-permute-start | bytes 73736 | tf_op jit(solution)/shard_map/ppermute | solution.py:163
  4.4 3.3 %collective-permute-start.2 = (bf16[8,1536]{1,0:T(8,128)(2,1)S(1)}, bf16[8,1536]{1,0:T(8,128)(2,1)S(1)}, u32[]{:S(2)}, u32[]{:S(2)}) collective-permute-start(bf16[8,1536]{1,0:T(8,128)(2,1)S(1)} %get-tuple-element.14), channel_id=1, source_target_pairs={{0,24},{8,16},{16,8},{24,0},{1,25},{9,17},{17,9},{25,1},{2,26},{10... | collective-permute-start | bytes 73736 | tf_op jit(solution)/shard_map/ppermute | solution.py:163
  9.2 9.0 %collective-permute-start.4 = (bf16[32,1536]{1,0:T(8,128)(2,1)S(1)}, bf16[32,1536]{1,0:T(8,128)(2,1)S(1)}, u32[]{:S(2)}, u32[]{:S(2)}) collective-permute-start(bf16[32,1536]{1,0:T(8,128)(2,1)S(1)} %up2.1), channel_id=1, source_target_pairs={{0,2},{1,3},{2,0},{3,1},{4,6},{5,7},{6,4},{7,5},{8,10},{9,11},{10,... | collective-permute-start | bytes 294920 | tf_op jit(solution)/shard_map/ppermute | solution.py:163
  13.4 14.2 %slice-start = ((s8[18874368]{0:T(1024)(128)(4,1)}), s8[4194304]{0:T(1024)(128)(4,1)S(1)}, s32[]{:S(2)}) async-start(s8[18874368]{0:T(1024)(128)(4,1)} %bitcast.10), calls=%async_computation.1 | async-start | bytes 8388608
  13.5 14.2 %slice-start.1 = ((s8[18874368]{0:T(1024)(128)(4,1)}), s8[4194304]{0:T(1024)(128)(4,1)S(1)}, s32[]{:S(2)}) async-start(s8[18874368]{0:T(1024)(128)(4,1)} %bitcast.10), calls=%async_computation.2 | async-start | bytes 8388608
  13.5 14.2 %slice-start.2 = ((s8[18874368]{0:T(1024)(128)(4,1)}), s8[4194304]{0:T(1024)(128)(4,1)S(1)}, s32[]{:S(2)}) async-start(s8[18874368]{0:T(1024)(128)(4,1)} %bitcast.10), calls=%async_computation.3 | async-start | bytes 8388608
  13.5 5.4 %collective-permute-start.5 = (bf16[32,1536]{1,0:T(8,128)(2,1)S(1)}, bf16[32,1536]{1,0:T(8,128)(2,1)S(1)}, u32[]{:S(2)}, u32[]{:S(2)}) collective-permute-start(bf16[32,1536]{1,0:T(8,128)(2,1)S(1)} %up1.1), channel_id=1, source_target_pairs={{0,1},{1,0},{2,3},{3,2},{4,5},{5,4},{6,7},{7,6},{8,9},{9,8},{10,11... | collective-permute-start | bytes 294920 | tf_op jit(solution)/shard_map/ppermute | solution.py:163
  16.6 11.1 %slice-start.3 = ((s8[18874368]{0:T(1024)(128)(4,1)}), s8[4194304]{0:T(1024)(128)(4,1)S(1)}, s32[]{:S(2)}) async-start(s8[18874368]{0:T(1024)(128)(4,1)} %bitcast.10), calls=%async_computation.4 | async-start | bytes 8388608
  16.6 11.0 %slice-start.4 = ((s8[18874368]{0:T(1024)(128)(4,1)}), s8[2097152]{0:T(1024)(128)(4,1)S(1)}, s32[]{:S(2)}) async-start(s8[18874368]{0:T(1024)(128)(4,1)} %bitcast.10), calls=%async_computation.5 | async-start | bytes 4194304
  16.6 6.5 %collective-permute-start.3 = (bf16[32,1536]{1,0:T(8,128)(2,1)S(1)}, bf16[32,1536]{1,0:T(8,128)(2,1)S(1)}, u32[]{:S(2)}, u32[]{:S(2)}) collective-permute-start(bf16[32,1536]{1,0:T(8,128)(2,1)S(1)} %up3.1), channel_id=1, source_target_pairs={{0,3},{1,2},{2,1},{3,0},{4,7},{5,6},{6,5},{7,4},{8,11},{9,10},{10,... | collective-permute-start | bytes 294920 | tf_op jit(solution)/shard_map/ppermute | solution.py:163
  23.2 5.4 %collective-permute-start.8 = (bf16[32,1536]{1,0:T(8,128)(2,1)S(1)}, bf16[32,1536]{1,0:T(8,128)(2,1)S(1)}, u32[]{:S(2)}, u32[]{:S(2)}) collective-permute-start(bf16[32,1536]{1,0:T(8,128)(2,1)S(1)} %act.1.refs_0_), channel_id=1, source_target_pairs={{0,1},{1,0},{2,3},{3,2},{4,5},{5,4},{6,7},{7,6},{8,9},{9,8},{10,11... | collective-permute-start | bytes 294920 | tf_op jit(solution)/shard_map/ppermute | solution.py:163
  24.0 9.1 %collective-permute-start.7 = (bf16[32,1536]{1,0:T(8,128)(2,1)S(1)}, bf16[32,1536]{1,0:T(8,128)(2,1)S(1)}, u32[]{:S(2)}, u32[]{:S(2)}) collective-permute-start(bf16[32,1536]{1,0:T(8,128)(2,1)S(1)} %act.1.refs_0_), channel_id=1, source_target_pairs={{0,2},{1,3},{2,0},{3,1},{4,6},{5,7},{6,4},{7,5},{8,10},{9,11},{10,... | collective-permute-start | bytes 294920 | tf_op jit(solution)/shard_map/ppermute | solution.py:163
  24.4 9.5 %collective-permute-start.6 = (bf16[32,1536]{1,0:T(8,128)(2,1)S(1)}, bf16[32,1536]{1,0:T(8,128)(2,1)S(1)}, u32[]{:S(2)}, u32[]{:S(2)}) collective-permute-start(bf16[32,1536]{1,0:T(8,128)(2,1)S(1)} %act.1.refs_0_), channel_id=1, source_target_pairs={{0,3},{1,2},{2,1},{3,0},{4,7},{5,6},{6,5},{7,4},{8,11},{9,10},{10,... | collective-permute-start | bytes 294920 | tf_op jit(solution)/shard_map/ppermute | solution.py:163
